TPU v7x, 32 devices: a whole 2x2x4 slice. The times are simulated.
32 devices in a mesh: dp: 8 (over z, x), head: 4 (over y, core).
Axes of the slice: x: 2, y: 2, z: 4, core: 2. Of those that a mesh axis runs over, the one named last changes fastest.
Arguments:
- residual: bfloat16 [32, 4096], P('dp', 'head'), may hold values from -6 to 6
- query: bfloat16 [32, 32, 128], P('dp', 'head'), may hold values from -4.5 to 4.5
- fresh_token_keys: bfloat16 [32, 8, 128], P('dp', 'head'), may hold values from -4.5 to 4.5
- value_new: bfloat16 [32, 8, 128], P('dp', 'head'), may hold values from -24 to 24
- key_cache: bfloat16 [32, 8, 2048, 128], P('dp', 'head'), may hold values from -6 to 6
- value_cache: bfloat16 [32, 8, 2048, 128], P('dp', 'head'), may hold values from -6 to 6
- lengths: int32 [32], P('dp'), may hold values from 1024 to 2048, as said below
- pages: int32 [32, 8, 64], P('dp', 'head'), may hold values from 0 to 127, as said below
- w_out: bfloat16 [4096, 4096], P('head', 'dp'), may hold values from -0.75 to 0.75
- norm_gain: float32 [4096], P('head'), may hold values from 0.5 to 1.5
- expert_ids: int32 [32, 2], P('dp'), may hold values from 0 to 7, all different within a row; in each aligned block of 4 rows (0 to 3, 4 to 7, ...) at most 2 rows name the same one
- gate_weights: float32 [32, 2], P('dp'), may hold values from 0.1 to 1
- w_in: bfloat16 [8, 2, 4096, 7168], P('dp', None, None, 'head'), may hold values from -0.09375 to 0.09375
- w_down: bfloat16 [8, 7168, 4096], P('dp', 'head'), may hold values from -0.0625 to 0.0625
Outputs:
- layer_out: bfloat16 [32, 4096], P('dp', 'head')
Inputs may be any that keep to these rules, and one draw needn't show every extreme that they name: `lengths`: each request's length; some request has exactly 2048 and some exactly 1024. `pages`: for each request and key head, 64 distinct page numbers, all below ceil(length / 16), always including the page that holds the request's last cached token; in no fixed order. `expert_ids`: per token 2 distinct experts; among the 4 tokens of one dp index no expert is named more than 2 times.
All inputs are finite; a program needn't handle non-finite values.
Results may differ from a plain program's by a relative error of at most 0.012.
Values may be sent and summed in bfloat16 or wider, within the bound.
A program may use at most 128 MiB of HBM per device.

v0:
```python
import jax
import jax.numpy as jnp
from jax import lax
from jax.sharding import PartitionSpec as P

EXPERTS = 8
TOP = 2
PAGE = 16
MOST = 2


EPSILON = 1e-05


def shards(
    residual,
    query,
    fresh_token_keys,
    value_new,
    key_cache,
    value_cache,
    lengths,
    pages,
    w_out,
    norm_gain,
    expert_ids,
    gate_weights,
    w_in,
    w_down,
):
    tok_rows = query.shape[0]
    head_local = query.shape[1]
    head_dim = query.shape[2]
    kv_local = key_cache.shape[1]
    cache_len = key_cache.shape[2]
    page_total = cache_len // PAGE
    group_member_count = head_local // kv_local
    page_numbers = jnp.arange(page_total, dtype=jnp.int32)
    page_chosen = jnp.any(pages[:, :, :, None] == page_numbers[None, None, None, :], axis=2)
    position_chosen = jnp.broadcast_to(
        page_chosen[:, :, :, None], (tok_rows, kv_local, page_total, PAGE)
    ).reshape(tok_rows, kv_local, cache_len)
    position_ids = jnp.arange(cache_len, dtype=jnp.int32)
    in_range = (position_chosen & (position_ids[None, None, :] < lengths[:, None, None]))[
        :, :, None, :
    ]
    grouped_rows = query.reshape(tok_rows, kv_local, group_member_count, head_dim)
    score_scale = head_dim ** (-0.5)
    scores = (
        jnp.einsum("bkgd,bksd->bkgs", grouped_rows, key_cache, preferred_element_type=jnp.float32)
        * score_scale
    )
    own_score = (
        jnp.einsum(
            "luxe,lue->lux", grouped_rows, fresh_token_keys, preferred_element_type=jnp.float32
        )
        * score_scale
    )
    masked = jnp.where(in_range, scores, -1e30)
    row_top = jnp.maximum(jnp.max(masked, axis=-1), own_score)
    expo = jnp.where(in_range, jnp.exp(scores - row_top[..., None]), 0.0)
    own_expo = jnp.exp(own_score - row_top)
    denominator = jnp.sum(expo, axis=-1) + own_expo
    weights = (expo / denominator[..., None]).astype(jnp.bfloat16)
    own_weight = (own_expo / denominator).astype(jnp.bfloat16)
    attended = jnp.einsum(
        "bkgs,bksd->bkgd", weights, value_cache, preferred_element_type=jnp.float32
    )
    attended = (
        attended
        + own_weight.astype(jnp.float32)[..., None] * value_new.astype(jnp.float32)[:, :, None, :]
    )
    attn_rows = attended.reshape(tok_rows, head_local * head_dim).astype(jnp.bfloat16)
    every_row = lax.all_gather(attn_rows, "dp", axis=0, tiled=True)
    column_part = jnp.dot(every_row, w_out, preferred_element_type=jnp.float32)
    head_partial = lax.all_to_all(
        column_part.astype(jnp.bfloat16), "dp", split_axis=0, concat_axis=1, tiled=True
    ).astype(column_part.dtype)
    stream = residual.astype(jnp.float32) + lax.psum_scatter(
        head_partial.astype(jnp.bfloat16), "head", scatter_dimension=1, tiled=True
    ).astype(jnp.float32)
    whole_stream, whole_gain = (
        lax.all_gather(stream, "head", axis=1, tiled=True),
        lax.all_gather(norm_gain, "head", axis=0, tiled=True),
    )
    square_mean_value = jnp.mean(whole_stream * whole_stream, axis=-1)
    normed = (
        whole_stream * lax.rsqrt(square_mean_value + EPSILON)[:, None] * whole_gain[None, :]
    ).astype(jnp.bfloat16)
    group_count = lax.axis_size("dp") // EXPERTS
    assignments = tok_rows * TOP
    flat_ids = expert_ids.reshape(assignments)
    expert_range = jnp.arange(EXPERTS, dtype=jnp.int32)
    onehot = (flat_ids[:, None] == expert_range[None, :]).astype(jnp.int32)
    earlier = jnp.cumsum(onehot, axis=0) - onehot
    slot_index = jnp.sum(earlier * onehot, axis=1)
    target = flat_ids * MOST + slot_index
    placement_map = jnp.arange(EXPERTS * MOST, dtype=jnp.int32)[:, None] == target[None, :]
    token_map = jnp.any(placement_map.reshape(EXPERTS * MOST, tok_rows, TOP), axis=2)
    outgoing = jnp.dot(
        token_map.astype(jnp.bfloat16), normed, preferred_element_type=jnp.float32
    ).astype(jnp.bfloat16)
    width_of_row = outgoing.shape[1]
    outgoing = jnp.broadcast_to(
        outgoing.reshape(EXPERTS, 1, MOST, width_of_row), (EXPERTS, group_count, MOST, width_of_row)
    )
    outgoing = outgoing.reshape(EXPERTS * group_count, MOST, width_of_row)
    arrived = lax.all_to_all(outgoing, "dp", split_axis=0, concat_axis=0, tiled=True)
    senders, slot_count, feature_count = arrived.shape
    flat_rows = arrived.reshape(senders * slot_count, feature_count)
    gate_act = jnp.dot(flat_rows, w_in[0, 0], preferred_element_type=jnp.float32)
    up_act = jnp.dot(flat_rows, w_in[0, 1], preferred_element_type=jnp.float32)
    hidden = (jax.nn.silu(gate_act) * up_act).astype(jnp.bfloat16)
    slab_out = jnp.dot(hidden, w_down[0], preferred_element_type=jnp.float32).reshape(
        senders, slot_count, w_down.shape[2]
    )
    summed_total = lax.psum_scatter(
        slab_out.astype(jnp.bfloat16), "head", scatter_dimension=2, tiled=True
    ).astype(jnp.float32)
    returned = lax.all_to_all(
        summed_total.astype(jnp.bfloat16), "dp", split_axis=0, concat_axis=0, tiled=True
    ).astype(summed_total.dtype)
    local_width = returned.shape[2]
    per_expert = jnp.sum(returned.reshape(EXPERTS, group_count, MOST, local_width), axis=1).reshape(
        EXPERTS * MOST, local_width
    )
    weighted = jnp.where(placement_map, gate_weights.reshape(assignments)[None, :], 0.0)
    combine_map = jnp.sum(weighted.reshape(EXPERTS * MOST, tok_rows, TOP), axis=2)
    mixture = jnp.dot(
        combine_map.T,
        per_expert,
        precision=lax.Precision.HIGHEST,
        preferred_element_type=jnp.float32,
    )
    return (stream + mixture).astype(jnp.bfloat16)


def solution(mesh):
    in_specs = (
        P("dp", "head"),
        P("dp", "head", None),
        P("dp", "head", None),
        P("dp", "head", None),
        P("dp", "head", None, None),
        P("dp", "head", None, None),
        P("dp"),
        P("dp", "head", None),
        P("head", "dp"),
        P("head"),
        P("dp", None),
        P("dp", None),
        P("dp", None, None, "head"),
        P("dp", "head", None),
    )
    out_specs = P("dp", "head")
    return jax.shard_map(shards, mesh=mesh, in_specs=in_specs, out_specs=out_specs, check_vma=False)
```

profile of v0, /device:TPU:0, one launch (start us, length us, event | category | flops | bytes accessed | tf_op | source)
XLA Modules:
  0.0 169.4 jit_solution(6646213300250157299)
XLA Ops:
  6.5 0.9 fusion.19
  7.5 0.2 broadcast_in_dim.28
  7.7 0.3 reshape.95
  8.0 0.7 iota_compare_fusion.1
  8.8 0.8 fusion.30
  9.6 3.5 %select_reduce_fusion = (f32[4,2,4]{2,1,0:T(2,128)S(1)}, f32[4,2,4,2048]{3,2,1,0:T(4,128)S(1)}) fusion(pred[4,2,2048]{2,1,0:T(4,128)(4,1)S(1)} %copy.32, bf16[4,2,4,128]{3,2,1,0:T(4,128)(2,1)} %bitcast.52, bf16[4,2,2048,128]{3,2,1,0:T(8,128)(2,1)} %param.18), kind=kOutput, calls=%fused_computation.19 | convolution fusion | flops 16973792 | bytes 4481152 | tf_op jit(solution)/shard_map/bkgd,bksd->bkgs/dot_general | solution.py:50
  13.1 0.3 fusion.20
  13.5 0.7 convert_element_type.55
  14.1 2.9 %fusion.18 = bf16[4,2,4,128]{3,2,1,0:T(4,128)(2,1)S(1)} fusion(bf16[4,2,2048,128]{3,2,1,0:T(8,128)(2,1)} %param.19, f32[4,2,4,2048]{3,2,1,0:T(4,128)S(1)} %get-tuple-element.8, f32[4,2,4]{2,1,0:T(2,128)S(1)} %get-tuple-element.6, f32[4,2,4]{2,1,0:T(2,128)S(1)} %multiply_maximum_fusion, pred[4,2,2048]{2,1,0:T(4,128)(4,1)S(1)} %copy.32, ...), kind=kOutput, calls=%fused_computation.17 | convolution fusion | flops 17051648 | bytes 4485504 | tf_op jit(solution)/shard_map/bkgs,bksd->bkgd/dot_general | solution.py:66
  17.1 32.4 %all-gather = bf16[8,4,1024]{2,1,0:T(4,128)(2,1)S(1)} all-gather(bf16[1,4,1024]{2,1,0:T(4,128)(2,1)S(1)} %reshape.99), channel_id=1, replica_groups=mesh['dp'=8,'head'=4] {'dp'}, dimensions={0}, use_global_device_ids=true | all-gather | bytes 73728 | tf_op jit(solution)/shard_map/all_gather | solution.py:74
  49.5 0.3 convolution_convert_fusion.1
  49.7 0.6 all_to_all.20
  50.4 5.5 %all-to-all-start = ((bf16[8,4,512]{2,1,0:T(4,128)(2,1)}), bf16[8,4,512]{2,1,0:T(4,128)(2,1)S(1)}, u32[]{:S(2)}, u32[]{:S(2)}) async-start(bf16[8,4,512]{2,1,0:T(4,128)(2,1)} %all_to_all.20), calls=%async_computation | async-start | bytes 65536 | tf_op jit(solution)/shard_map/all_to_all | solution.py:76
  55.9 0.8 copy.33
  56.8 0.2 select_reduce_fusion.2
  57.2 5.3 %all_gather.11 = f32[4096]{0:T(1024)S(1)} all-gather(f32[1024]{0:T(1024)} %param.23), channel_id=1, replica_groups=mesh['dp'=8,'head'=4] {'head'}, dimensions={0}, use_global_device_ids=true | all-gather | bytes 20480 | tf_op jit(solution)/shard_map/all_gather | solution.py:84
  62.6 1.4 copy.40
  64.1 26.2 %reduce-scatter.7.cloned.1.call-done = bf16[1024,4]{1,0:T(8,128)(2,1)} async-done(((bf16[4096,4]{1,0:T(8,128)(2,1)}), bf16[1024,4]{1,0:T(8,128)(2,1)}) %reduce-scatter.7.cloned.1.call-update) | async-done | bytes 8208
  90.3 1.1 copy.41
  91.4 0.7 convert_add_fusion
  92.1 5.2 %all_gather.10 = f32[4,4096]{1,0:T(4,128)S(1)} all-gather(f32[4,1024]{1,0:T(4,128)S(1)} %convert_add_fusion), channel_id=1, replica_groups=mesh['dp'=8,'head'=4] {'head'}, dimensions={1}, use_global_device_ids=true | all-gather | bytes 81920 | tf_op jit(solution)/shard_map/all_gather | solution.py:83
  97.3 0.1 multiply_reduce_fusion
  97.5 0.3 convolution_convert_fusion
  97.8 12.8 %all_to_all.29 = bf16[8,2,4096]{2,1,0:T(2,128)(2,1)S(1)} all-to-all(bf16[8,2,4096]{2,1,0:T(2,128)(2,1)S(1)} %reshape_reshape.3), channel_id=1, replica_groups=mesh['dp'=8,'head'=4] {'dp'}, dimensions={0} | all-to-all | bytes 262144 | tf_op jit(solution)/shard_map/all_to_all | solution.py:108
  110.7 6.2 %fusion.4 = f32[16,1792]{1,0:T(8,128)S(1)} fusion(bf16[16,4096]{1,0:T(8,128)(2,1)S(1)} %reshape.97, bf16[1,2,4096,1792]{3,2,1,0:T(8,128)(2,1)} %param.26), kind=kOutput, calls=%fused_computation.4 | convolution fusion | flops 234881024 | bytes 14925824 | tf_op jit(solution)/shard_map/dot_general | solution.py:111
  117.0 6.3 %fusion.14 = bf16[16,1792]{1,0:T(8,128)(2,1)S(1)} fusion(bf16[16,4096]{1,0:T(8,128)(2,1)S(1)} %reshape.97, bf16[1,2,4096,1792]{3,2,1,0:T(8,128)(2,1)} %param.26, f32[16,1792]{1,0:T(8,128)S(1)} %fusion.4), kind=kOutput, calls=%fused_computation.12 | convolution fusion | flops 235053056 | bytes 14983168 | tf_op jit(solution)/shard_map/dot_general | solution.py:112
  123.3 7.8 %fusion.8 = bf16[8,2,4096]{2,0,1:T(8,128)(2,1)} fusion(bf16[1,1792,4096]{2,1,0:T(8,128)(2,1)} %param.27, bf16[8,2,1792]{2,1,0:T(2,128)(2,1)S(1)} %dot_general.36), kind=kOutput, calls=%fused_computation.8 | convolution fusion | flops 234946560 | bytes 14868480 | tf_op jit(solution)/shard_map/dot_general | solution.py:114
  131.2 17.0 %reduce-scatter.5.cloned.1.call-done = bf16[8,2,1024]{2,0,1:T(8,128)(2,1)} async-done(((bf16[8,2,4096]{2,0,1:T(8,128)(2,1)}), bf16[8,2,1024]{2,0,1:T(8,128)(2,1)}) %reduce-scatter.5.cloned.1.call-update) | async-done | bytes 32784 | tf_op jit(solution)/shard_map/reduce_scatter | solution.py:117
  148.2 1.4 copy.37
  149.6 5.5 %all-to-all-start.2 = ((bf16[8,2,1024]{2,1,0:T(2,128)(2,1)}), bf16[8,2,1024]{2,1,0:T(2,128)(2,1)S(1)}, u32[]{:S(2)}, u32[]{:S(2)}) async-start(bf16[8,2,1024]{2,1,0:T(2,128)(2,1)} %copy.37), calls=%async_computation.3 | async-start | bytes 65536 | tf_op jit(solution)/shard_map/all_to_all | solution.py:120
  155.2 6.6 %all-to-all-done.2 = bf16[8,2,1024]{2,1,0:T(2,128)(2,1)S(1)} async-done(((bf16[8,2,1024]{2,1,0:T(2,128)(2,1)}), bf16[8,2,1024]{2,1,0:T(2,128)(2,1)S(1)}, u32[]{:S(2)}, u32[]{:S(2)}) %all-to-all-start.2) | async-done | bytes 32800 | tf_op jit(solution)/shard_map/all_to_all | solution.py:120
  161.8 0.7 fusion.17
  (32 shorter events, 1.0 us)
Async XLA Ops:
  6.5 42.9 %copy-start = (bf16[1024,512]{1,0:T(8,128)(2,1)S(1)}, bf16[1024,512]{1,0:T(8,128)(2,1)}, u32[]{:S(2)}) copy-start(bf16[1024,512]{1,0:T(8,128)(2,1)} %param.22) | copy-start | bytes 3145732
  50.4 12.2 %all-to-all-start = ((bf16[8,4,512]{2,1,0:T(4,128)(2,1)}), bf16[8,4,512]{2,1,0:T(4,128)(2,1)S(1)}, u32[]{:S(2)}, u32[]{:S(2)}) async-start(bf16[8,4,512]{2,1,0:T(4,128)(2,1)} %all_to_all.20), calls=%async_computation | async-start | bytes 65536 | tf_op jit(solution)/shard_map/all_to_all | solution.py:76
  55.8 34.5 %reduce-scatter.7.cloned.1.call-start = ((), (), s32[]{:S(2)}) async-start(), calls=%async_computation.6 | async-start | bytes 1310720
  64.0 84.2 %reduce-scatter.5.cloned.1.call-start = ((), (), s32[]{:S(2)}) async-start(), calls=%async_computation.5 | async-start | bytes 163840 | tf_op jit(solution)/shard_map/reduce_scatter | solution.py:117
  117.0 38.1 %copy-start.2 = (f32[4,2]{0,1:T(2,128)S(1)}, f32[4,2]{0,1:T(2,128)}, u32[]{:S(2)}) copy-start(f32[4,2]{0,1:T(2,128)} %param.25) | copy-start | bytes 100
  117.0 44.8 %copy-start.1 = (bf16[4,1024]{1,0:T(4,128)(2,1)S(1)}, bf16[4,1024]{1,0:T(4,128)(2,1)}, u32[]{:S(2)}) copy-start(bf16[4,1024]{1,0:T(4,128)(2,1)} %param.14) | copy-start | bytes 24580
  149.6 12.2 %all-to-all-start.2 = ((bf16[8,2,1024]{2,1,0:T(2,128)(2,1)}), bf16[8,2,1024]{2,1,0:T(2,128)(2,1)S(1)}, u32[]{:S(2)}, u32[]{:S(2)}) async-start(bf16[8,2,1024]{2,1,0:T(2,128)(2,1)} %copy.37), calls=%async_computation.3 | async-start | bytes 65536 | tf_op jit(solution)/shard_map/all_to_all | solution.py:120
Sparse Core Ops, SparseCore 0:
  64.1 26.1 reduce-scatter.6
  131.3 16.8 reduce-scatter.4
where the time goes:
time: 170 us; the launch traced here: 169 us
  blocking collectives  55.7 us (33%)
  waiting for transfers between devices  49.8 us (29%)
  matrix products  28.9 us (17%)
  between operations  13.6 us (8%)
  starting transfers between devices  11.1 us (7%)
  local copies, waits for them, and re-layouts  6.35 us (4%)
  other arithmetic  4 us (2%)
    all_gather x1, blocking collectives, shards(): every_row = lax.all_gather(attn_rows, 'dp', axis=0, tiled=True)  32.4 us
    unnamed x3, waiting for transfers between devices  26.2 us
    reduce_scatter x1, waiting for transfers between devices, shards(): lax.psum_scatter(slab_out.astype(jnp.bfloat16), 'head', scatter_dimension...  17 us
    all_to_all x1, blocking collectives, shards(): lax.all_to_all(outgoing, 'dp', split_axis=0, concat_axis=0, tiled=True)  12.8 us
    dot_general x1, matrix products, shards(): jnp.dot(hidden, w_down[0], preferred_element_type=jnp.float32)  7.82 us
    all_to_all x1, waiting for transfers between devices, shards(): lax.all_to_all(summed_total.astype(jnp.bfloat16), 'dp', split_axis=0, con...  6.6 us
    dot_general x1, matrix products, shards(): up_act = jnp.dot(flat_rows, w_in[0, 1], preferred_element_type=jnp.float32)  6.3 us
    dot_general x1, matrix products, shards(): jnp.dot(flat_rows, w_in[0, 0], preferred_element_type=jnp.float32)  6.24 us
  transfers between devices with their start and end apart: 4, of which 3 were waited for; matrix products, arithmetic and copies ran while one was open for 1% of the time, Pallas kernels for 0%

commit v1 on v0

v1 whole, which is shorter than its diff:
```python
import functools

import jax
import jax.numpy as jnp
from jax import lax
from jax.experimental import pallas as pl
from jax.experimental.pallas import tpu as pltpu
from jax.sharding import PartitionSpec as P

EXPERTS = 8
PAGE = 16
EPSILON = 1e-05
LANES = 128
TILE = 256
MESH = pl.DeviceIdType.MESH


def hidden_tile(width):
    return TILE if width % TILE == 0 else width


def layer_kernel(
    nd,
    nh,
    residual_ref,
    query_ref,
    fresh_ref,
    value_new_ref,
    lengths_ref,
    pages_ref,
    gain_ref,
    ids_ref,
    gates_ref,
    key_hbm,
    value_hbm,
    w_out_hbm,
    w_in_hbm,
    w_down_hbm,
    out_ref,
    keys,
    values,
    w_out,
    w_in,
    w_down,
    attn,
    residual_all,
    routing_all,
    rows_all,
    gain_all,
    partial_all,
    stream_all,
    lhs,
    block,
    routing,
    normed,
    hidden,
    slab_send,
    slab_recv,
    total,
    own_stream,
    back_send,
    back_recv,
    cache_sem,
    w_out_sem,
    w_in_sem,
    w_down_sem,
    dp_send,
    dp_recv,
    head_send,
    head_recv,
):
    d, h = lax.axis_index("dp"), lax.axis_index("head")
    rows, heads, head_dim = query_ref.shape
    kv = key_hbm.shape[1]
    cache_len = key_hbm.shape[2]
    members = heads // kv
    tokens = nd * rows
    per_head = residual_ref.shape[1]
    per_dp = w_out.shape[1]
    width = w_down_hbm.shape[2]
    tiles, _, _, tile = w_in.shape
    experts_per = nd // EXPERTS
    page_total = cache_len // PAGE

    cache_copies = []
    for b in range(rows):
        pair = (
            pltpu.make_async_copy(key_hbm.at[b], keys.at[b], cache_sem.at[0, b]),
            pltpu.make_async_copy(value_hbm.at[b], values.at[b], cache_sem.at[1, b]),
        )
        pair[0].start()
        pair[1].start()
        cache_copies.append(pair)
    w_out_copy = pltpu.make_async_copy(w_out_hbm, w_out, w_out_sem)
    w_out_copy.start()

    def w_in_copy(n):
        start = n * tile if isinstance(n, int) else pl.multiple_of(n * tile, tile)
        return pltpu.make_async_copy(
            w_in_hbm.at[0, :, :, pl.ds(start, tile)], w_in.at[n], w_in_sem.at[n]
        )

    for n in range(tiles):
        w_in_copy(n).start()
    down_copies = []
    for k in range(nh):
        owner = lax.rem(h + (k + 1) % nh, nh)
        copy = pltpu.make_async_copy(
            w_down_hbm.at[0, :, pl.ds(pl.multiple_of(owner * per_head, LANES), per_head)],
            w_down.at[k],
            w_down_sem.at[k],
        )
        copy.start()
        down_copies.append(copy)

    def dp_peer(r):
        return (lax.rem(d + r, nd), h)

    def head_peer(r):
        return (d, lax.rem(h + r, nh))

    barrier = pltpu.get_barrier_semaphore()
    for r in range(1, nd):
        pl.semaphore_signal(barrier, inc=1, device_id=dp_peer(r), device_id_type=MESH)
    for r in range(1, nh):
        pl.semaphore_signal(barrier, inc=1, device_id=head_peer(r), device_id_type=MESH)

    lane = lax.broadcasted_iota(jnp.int32, (rows, LANES), 1)
    mine = jnp.zeros((rows, LANES), jnp.float32)
    for j in range(ids_ref.shape[1]):
        mine = mine + jnp.where(ids_ref[:, j : j + 1] == lane, gates_ref[:, j : j + 1], 0.0)
    routing_all[d] = mine
    residual_all[d] = residual_ref[...]
    gain_all[h] = gain_ref[...]

    pl.semaphore_wait(barrier, nd + nh - 2)

    pending = []

    def over_dp(stage, source, target):
        copies = []
        for r in range(1, nd):
            copy = pltpu.make_async_remote_copy(
                src_ref=source(r),
                dst_ref=target,
                send_sem=dp_send.at[stage, r],
                recv_sem=dp_recv.at[stage, r],
                device_id=dp_peer(r),
                device_id_type=MESH,
            )
            copy.start()
            copies.append(copy)
        pending.extend(copies)
        return copies

    def to_head(stage, r, source, target):
        copy = pltpu.make_async_remote_copy(
            src_ref=source,
            dst_ref=target,
            send_sem=head_send.at[stage, r],
            recv_sem=head_recv.at[stage, r],
            device_id=head_peer(r),
            device_id_type=MESH,
        )
        copy.start()
        pending.append(copy)
        return copy

    def arrived(copies):
        for copy in copies:
            copy.wait_recv()

    residual_copies = over_dp(0, lambda r: residual_ref, residual_all.at[d])
    routing_copies = over_dp(1, lambda r: routing_all.at[d], routing_all.at[d])
    gain_copies = [to_head(0, r, gain_ref, gain_all.at[h]) for r in range(1, nh)]

    group_of_row = lax.broadcasted_iota(jnp.int32, (heads, 1), 0) // members

    def by_group(parts):
        chosen = parts[0]
        for k in range(1, kv):
            chosen = jnp.where(group_of_row == k, parts[k], chosen)
        return chosen

    position = lax.broadcasted_iota(jnp.int32, (1, cache_len), 1)
    spread = (
        lax.broadcasted_iota(jnp.int32, (page_total, cache_len), 1) // PAGE
        == lax.broadcasted_iota(jnp.int32, (page_total, cache_len), 0)
    )
    spread = jnp.where(spread, 1.0, 0.0).astype(jnp.bfloat16)
    scale = head_dim ** (-0.5)
    page_shape = (kv, pages_ref.shape[2], page_total)
    page_number = lax.broadcasted_iota(jnp.int32, page_shape, 2)
    for b in range(rows):
        named = jnp.where(pages_ref[b][:, :, None] == page_number, 1.0, 0.0)
        named = jnp.max(named, axis=1)
        named = by_group([named[k : k + 1, :] for k in range(kv)])
        named = jnp.broadcast_to(named, (heads, page_total)).astype(jnp.bfloat16)
        chosen = jnp.dot(named, spread, preferred_element_type=jnp.float32)
        live = (chosen > 0.5) & (position < lengths_ref[b])
        q = query_ref[b]
        fresh = fresh_ref[b].astype(jnp.float32)
        fresh = by_group([fresh[k : k + 1, :] for k in range(kv)])
        own = jnp.sum(q.astype(jnp.float32) * fresh, axis=1, keepdims=True) * scale
        cache_copies[b][0].wait()
        score = by_group(
            [
                lax.dot_general(
                    q,
                    keys[b, k],
                    (((1,), (1,)), ((), ())),
                    preferred_element_type=jnp.float32,
                )
                for k in range(kv)
            ]
        )
        score = jnp.where(live, score * scale, -1e30)
        top = jnp.maximum(jnp.max(score, axis=1, keepdims=True), own)
        expo = jnp.where(live, jnp.exp(score - top), 0.0)
        own_expo = jnp.exp(own - top)
        inverse = 1.0 / (jnp.sum(expo, axis=1, keepdims=True) + own_expo)
        weights = (expo * inverse).astype(jnp.bfloat16)
        own_weight = (own_expo * inverse).astype(jnp.bfloat16).astype(jnp.float32)
        cache_copies[b][1].wait()
        mixed = by_group(
            [
                jnp.dot(weights, values[b, k], preferred_element_type=jnp.float32)
                for k in range(kv)
            ]
        )
        newest = value_new_ref[b].astype(jnp.float32)
        newest = by_group([newest[k : k + 1, :] for k in range(kv)])
        attn[b * heads : (b + 1) * heads, :] = mixed + own_weight * newest

    for x in range(heads):
        rows_all[d, :, x * head_dim : (x + 1) * head_dim] = attn[pl.ds(x, rows, stride=heads), :]
    rows_copies = over_dp(2, lambda r: rows_all.at[d], rows_all.at[d])

    arrived(residual_copies)
    first = d * per_dp
    offset = pl.multiple_of(lax.rem(first, per_head), LANES)
    holds = jnp.where(first // per_head == h, 1.0, 0.0)
    for i in range(nd):
        piece = residual_all[i, :, pl.ds(offset, per_dp)].astype(jnp.float32)
        block[i * rows : (i + 1) * rows, :] = piece * holds

    w_out_copy.wait()
    arrived(rows_copies)
    for i in range(nd):
        lhs[i * rows : (i + 1) * rows, :] = rows_all[i]
    partial = block[...] + jnp.dot(
        lhs[...].astype(jnp.bfloat16), w_out[...], preferred_element_type=jnp.float32
    )
    partial_all[h] = partial.astype(jnp.bfloat16)
    partial_copies = [
        to_head(1, r, partial_all.at[h], partial_all.at[h]) for r in range(1, nh)
    ]
    arrived(partial_copies)
    stream = partial_all[0].astype(jnp.float32)
    for i in range(1, nh):
        stream = stream + partial_all[i].astype(jnp.float32)
    stream_all[d] = stream.astype(jnp.bfloat16)
    stream_copies = over_dp(3, lambda r: stream_all.at[d], stream_all.at[d])

    arrived(routing_copies)
    for i in range(nd):
        routing[i * rows : (i + 1) * rows, :] = routing_all[i]
    lane = lax.broadcasted_iota(jnp.int32, (tokens, LANES), 1)
    weight = jnp.sum(
        jnp.where(lane == d // experts_per, routing[...], 0.0), axis=1, keepdims=True
    )
    arrived(gain_copies)

    arrived(stream_copies)
    squares = jnp.zeros((tokens, 1), jnp.float32)
    for i in range(nd):
        piece = stream_all[i].astype(jnp.float32)
        squares = squares + jnp.sum(piece * piece, axis=1, keepdims=True)
    factor = lax.rsqrt(squares / width + EPSILON)
    for i in range(nd):
        start = i * per_dp
        at = start % per_head
        gain = gain_all[start // per_head, :, at : at + per_dp]
        piece = stream_all[i].astype(jnp.float32) * factor * gain
        normed[:, start : start + per_dp] = piece.astype(jnp.bfloat16)

    def hidden_step(n):
        w_in_copy(n).wait()
        gate_act = jnp.dot(normed[...], w_in[n, 0], preferred_element_type=jnp.float32)
        up_act = jnp.dot(normed[...], w_in[n, 1], preferred_element_type=jnp.float32)
        start = 0 if tiles == 1 else pl.multiple_of(n * tile, tile)
        act = gate_act * jax.nn.sigmoid(gate_act) * up_act
        hidden[:, pl.ds(start, tile)] = act.astype(jnp.bfloat16)

    if tiles == 1:
        hidden_step(0)
    else:
        pl.loop(0, tiles)(hidden_step)

    slab_copies = []
    for k in range(nh):
        down_copies[k].wait()

        @pl.loop(0, per_head // TILE)
        def _(c, k=k):
            columns = pl.ds(pl.multiple_of(c * TILE, TILE), TILE)
            piece = weight * jnp.dot(
                hidden[...], w_down[k, :, columns], preferred_element_type=jnp.float32
            )
            if k < nh - 1:
                slab_send[k, :, columns] = piece.astype(jnp.bfloat16)
            else:
                total[:, columns] = piece

        if k < nh - 1:
            slab_copies.append(to_head(2, k + 1, slab_send.at[k], slab_recv.at[k]))

    for j in range(per_head // per_dp):
        piece = stream_all[h * (per_head // per_dp) + j].astype(jnp.float32)
        for i in range(nd):
            own_stream[i, :, j * per_dp : (j + 1) * per_dp] = piece[i * rows : (i + 1) * rows, :]

    arrived(slab_copies)
    summed = total[...]
    for k in range(nh - 1):
        summed = summed + slab_recv[k].astype(jnp.float32)
    for i in range(nd):
        back_send[i] = summed[i * rows : (i + 1) * rows, :]
    back_copies = over_dp(4, lambda r: back_send.at[lax.rem(d + r, nd)], back_recv.at[d])
    result = own_stream[d] + back_send[d]
    arrived(back_copies)
    for r in range(1, nd):
        result = result + back_recv[lax.rem(d + nd - r, nd)]
    out_ref[...] = result.astype(out_ref.dtype)
    for copy in pending:
        copy.wait_send()


def shards(
    nd,
    nh,
    residual,
    query,
    fresh_token_keys,
    value_new,
    key_cache,
    value_cache,
    lengths,
    pages,
    w_out,
    norm_gain,
    expert_ids,
    gate_weights,
    w_in,
    w_down,
):
    rows, heads, head_dim = query.shape
    per_head = residual.shape[1]
    per_dp = w_out.shape[1]
    tokens = nd * rows
    deep, units = w_in.shape[2], w_in.shape[3]
    tile = hidden_tile(units)
    f32, bf16 = jnp.float32, jnp.bfloat16
    vmem = pl.BlockSpec(memory_space=pltpu.VMEM)
    smem = pl.BlockSpec(memory_space=pltpu.SMEM)
    hbm = pl.BlockSpec(memory_space=pl.ANY)
    scratch = [
        pltpu.VMEM(key_cache.shape, bf16),
        pltpu.VMEM(value_cache.shape, bf16),
        pltpu.VMEM(w_out.shape, bf16),
        pltpu.VMEM((units // tile, 2, deep, tile), bf16),
        pltpu.VMEM((nh, units, per_head), bf16),
        pltpu.VMEM((rows * heads, head_dim), f32),
        pltpu.VMEM((nd, rows, per_head), bf16),
        pltpu.VMEM((nd, rows, LANES), f32),
        pltpu.VMEM((nd, rows, heads * head_dim), f32),
        pltpu.VMEM((nh, 1, per_head), f32),
        pltpu.VMEM((nh, tokens, per_dp), bf16),
        pltpu.VMEM((nd, tokens, per_dp), bf16),
        pltpu.VMEM((tokens, heads * head_dim), f32),
        pltpu.VMEM((tokens, per_dp), f32),
        pltpu.VMEM((tokens, LANES), f32),
        pltpu.VMEM((tokens, deep), bf16),
        pltpu.VMEM((tokens, units), bf16),
        pltpu.VMEM((nh - 1, tokens, per_head), bf16),
        pltpu.VMEM((nh - 1, tokens, per_head), bf16),
        pltpu.VMEM((tokens, per_head), f32),
        pltpu.VMEM((nd, rows, per_head), f32),
        pltpu.VMEM((nd, rows, per_head), f32),
        pltpu.VMEM((nd, rows, per_head), f32),
        pltpu.SemaphoreType.DMA((2, rows)),
        pltpu.SemaphoreType.DMA,
        pltpu.SemaphoreType.DMA((units // tile,)),
        pltpu.SemaphoreType.DMA((nh,)),
        pltpu.SemaphoreType.DMA((5, nd)),
        pltpu.SemaphoreType.DMA((5, nd)),
        pltpu.SemaphoreType.DMA((3, nh)),
        pltpu.SemaphoreType.DMA((3, nh)),
    ]
    return pl.pallas_call(
        functools.partial(layer_kernel, nd, nh),
        out_shape=jax.ShapeDtypeStruct(residual.shape, bf16),
        in_specs=[vmem] * 4 + [smem] + [vmem] * 4 + [hbm] * 5,
        out_specs=vmem,
        scratch_shapes=scratch,
        compiler_params=pltpu.CompilerParams(
            collective_id=0, has_side_effects=True, vmem_limit_bytes=65_000_000
        ),
    )(
        residual,
        query,
        fresh_token_keys,
        value_new,
        lengths,
        pages,
        norm_gain.reshape(1, -1),
        expert_ids,
        gate_weights,
        key_cache,
        value_cache,
        w_out,
        w_in,
        w_down,
    )


def solution(mesh):
    in_specs = (
        P("dp", "head"),
        P("dp", "head", None),
        P("dp", "head", None),
        P("dp", "head", None),
        P("dp", "head", None, None),
        P("dp", "head", None, None),
        P("dp"),
        P("dp", "head", None),
        P("head", "dp"),
        P("head"),
        P("dp", None),
        P("dp", None),
        P("dp", None, None, "head"),
        P("dp", "head", None),
    )
    body = functools.partial(shards, mesh.shape["dp"], mesh.shape["head"])
    return jax.shard_map(
        body, mesh=mesh, in_specs=in_specs, out_specs=P("dp", "head"), check_vma=False
    )
```

time: 170 us -> 56.4 us (0.33)
  blocking collectives: 55.7 us -> 0 us
  Pallas kernels: 0 us -> 52.2 us
  waiting for transfers between devices: 49.8 us -> 0 us
  matrix products: 28.9 us -> 0 us
  between operations: 13.6 us -> 0.01 us
  starting transfers between devices: 11.1 us -> 0 us
  other arithmetic: 4 us -> 0 us
  local copies, waits for them, and re-layouts: 6.35 us -> 3.98 us
    pallas_call x0 -> x1, Pallas kernels: none -> 52.2 us  [shards(): pl.pallas_call(functools.partial(layer_kernel, nd, nh), out_shape=jax.Sha...]
    all_gather x3 -> x0, blocking collectives: 42.9 us -> none  [the longest x1 32.4 us: shards(): every_row = lax.all_gather(attn_rows, 'dp', axis=0, tiled=True)]
    dot_general x9 -> x0, matrix products: 28.9 us -> none  [the longest x1 7.82 us: shards(): jnp.dot(hidden, w_down[0], preferred_element_type=jnp.float32)]
    unnamed x3 -> x0, waiting for transfers between devices: 26.2 us -> none
    reduce_scatter x1 -> x0, waiting for transfers between devices: 17 us -> none  [shards(): lax.psum_scatter(slab_out.astype(jnp.bfloat16), 'head', scatter_dimension...]
    all_to_all x1 -> x0, blocking collectives: 12.8 us -> none  [shards(): lax.all_to_all(outgoing, 'dp', split_axis=0, concat_axis=0, tiled=True)]
    all_to_all x2 -> x0, starting transfers between devices: 11 us -> none  [the longest x1 5.51 us: shards(): lax.all_to_all(summed_total.astype(jnp.bfloat16), 'dp', split_axis=0, con...]
    all_to_all x2 -> x0, waiting for transfers between devices: 6.6 us -> none  [the longest x1 6.6 us: shards(): lax.all_to_all(summed_total.astype(jnp.bfloat16), 'dp', split_axis=0, con...]
  transfers between devices with their start and end apart: 4 -> 0, of which waited for: 3 -> 0; matrix products, arithmetic and copies ran while one was open for 1% -> 0% of each run, Pallas kernels for 0% -> 0%
where the time goes in v1:
time: 56.4 us; the launch traced here: 56.1 us
  Pallas kernels  52.2 us (93%)
  local copies, waits for them, and re-layouts  3.98 us (7%)
    pallas_call x1, Pallas kernels, shards(): pl.pallas_call(functools.partial(layer_kernel, nd, nh), out_shape=jax.Sha...  52.2 us
    unnamed x3, local copies, waits for them, and re-layouts  3.98 us

profile of v1, /device:TPU:0, one launch (start us, length us, event | category | flops | bytes accessed | tf_op | source)
XLA Modules:
  0.0 56.1 jit_solution(3154734190532949285)
XLA Ops:
  0.0 1.3 %copy.15.ids_ref = s32[4,2]{1,0:T(4,128)} copy(s32[4,2]{0,1:T(2,128)} %param.24) | data formatting | bytes 64 | tf_op args[10]
  1.3 1.3 %copy.16.gates_ref = f32[4,2]{1,0:T(4,128)} copy(f32[4,2]{0,1:T(2,128)} %param.25) | data formatting | bytes 64 | tf_op args[11]
  2.7 52.2 %shard_map.136 = bf16[4,1024]{1,0:T(4,128)(2,1)} custom-call(bf16[4,1024]{1,0:T(4,128)(2,1)} %residual_ref.1, bf16[4,8,128]{2,1,0:T(8,128)(2,1)} %query_ref.1, bf16[4,2,128]{2,1,0:T(2,128)(2,1)} %fresh_ref.1, bf16[4,2,128]{2,1,0:T(2,128)(2,1)} %value_new_ref.1, s32[4]{0:T(128)} %lengths_ref.1, s32[4,2,64]{2,1,0:T(2,128)} %pages_ref.1, f32[1,1024]{1,0:T(1,128)} %bitcast.1, ...), custom_call_target="tpu_custom_call" | custom-call | tf_op jit(solution)/shard_map/pallas_call | solution.py:400
  54.8 1.3 %copy.18 = bf16[4,1024]{1,0:T(4,128)(2,1)} copy(bf16[4,1024]{1,0:T(4,128)(2,1)} %shard_map.136) | data formatting | bytes 16384

commit v2 on v1

--- a/solution.py
+++ b/solution.py
@@ -47,6 +47,7 @@
     routing_all,
     rows_all,
     gain_all,
+    partial_send,
     partial_all,
     stream_all,
     lhs,
@@ -68,6 +69,8 @@
     dp_recv,
     head_send,
     head_recv,
+    pair_send,
+    pair_recv,
 ):
     d, h = lax.axis_index("dp"), lax.axis_index("head")
     rows, heads, head_dim = query_ref.shape
@@ -77,6 +80,7 @@
     tokens = nd * rows
     per_head = residual_ref.shape[1]
     per_dp = w_out.shape[1]
+    parts, _, _, part = stream_all.shape
     width = w_down_hbm.shape[2]
     tiles, _, _, tile = w_in.shape
     experts_per = nd // EXPERTS
@@ -101,7 +105,7 @@
         )
 
     for n in range(tiles):
-        w_in_copy(n).start()
+        w_in_copy(n).start(priority=1)
     down_copies = []
     for k in range(nh):
         owner = lax.rem(h + (k + 1) % nh, nh)
@@ -110,7 +114,7 @@
             w_down.at[k],
             w_down_sem.at[k],
         )
-        copy.start()
+        copy.start(priority=1)
         down_copies.append(copy)
 
     def dp_peer(r):
@@ -127,8 +131,11 @@
 
     lane = lax.broadcasted_iota(jnp.int32, (rows, LANES), 1)
     mine = jnp.zeros((rows, LANES), jnp.float32)
-    for j in range(ids_ref.shape[1]):
-        mine = mine + jnp.where(ids_ref[:, j : j + 1] == lane, gates_ref[:, j : j + 1], 0.0)
+    row = lax.broadcasted_iota(jnp.int32, (rows, LANES), 0)
+    for j in range(ids_ref.shape[0]):
+        for t in range(rows):
+            named = (row == t) & (lane == ids_ref[j, t])
+            mine = mine + jnp.where(named, gates_ref[j, t], 0.0)
     routing_all[d] = mine
     residual_all[d] = residual_ref[...]
     gain_all[h] = gain_ref[...]
@@ -233,7 +240,8 @@
         attn[b * heads : (b + 1) * heads, :] = mixed + own_weight * newest
 
     for x in range(heads):
-        rows_all[d, :, x * head_dim : (x + 1) * head_dim] = attn[pl.ds(x, rows, stride=heads), :]
+        head_rows = attn[pl.ds(x, rows, stride=heads), :]
+        rows_all[d, :, x * head_dim : (x + 1) * head_dim] = head_rows.astype(jnp.bfloat16)
     rows_copies = over_dp(2, lambda r: rows_all.at[d], rows_all.at[d])
 
     arrived(residual_copies)
@@ -247,20 +255,41 @@
     w_out_copy.wait()
     arrived(rows_copies)
     for i in range(nd):
-        lhs[i * rows : (i + 1) * rows, :] = rows_all[i]
+        lhs[i * rows : (i + 1) * rows, :] = rows_all[i].astype(jnp.float32)
     partial = block[...] + jnp.dot(
         lhs[...].astype(jnp.bfloat16), w_out[...], preferred_element_type=jnp.float32
     )
-    partial_all[h] = partial.astype(jnp.bfloat16)
+    for c in range(parts):
+        partial_send[c] = partial[:, c * part : (c + 1) * part].astype(jnp.bfloat16)
     partial_copies = [
-        to_head(1, r, partial_all.at[h], partial_all.at[h]) for r in range(1, nh)
+        to_head(1, r, partial_send.at[lax.rem(h + r, parts)], partial_all.at[h])
+        for r in range(1, nh)
     ]
+    mine_of = lax.rem(h, parts)
+    partial_all[h] = partial_send[mine_of]
     arrived(partial_copies)
     stream = partial_all[0].astype(jnp.float32)
     for i in range(1, nh):
         stream = stream + partial_all[i].astype(jnp.float32)
-    stream_all[d] = stream.astype(jnp.bfloat16)
-    stream_copies = over_dp(3, lambda r: stream_all.at[d], stream_all.at[d])
+    stream_all[mine_of, d] = stream.astype(jnp.bfloat16)
+    stream_copies = over_dp(3, lambda r: stream_all.at[mine_of, d], stream_all.at[mine_of, d])
+    partner = h + 1 - 2 * lax.rem(h, 2)
+
+    def forward(r):
+        piece = stream_all.at[mine_of, lax.rem(d + nd - r, nd)]
+        copy = pltpu.make_async_remote_copy(
+            src_ref=piece,
+            dst_ref=piece,
+            send_sem=pair_send.at[r],
+            recv_sem=pair_recv.at[r],
+            device_id=(d, partner),
+            device_id_type=MESH,
+        )
+        copy.start()
+        pending.append(copy)
+        return copy
+
+    pair_copies = [forward(0)] if parts == 2 else []
 
     arrived(routing_copies)
     for i in range(nd):
@@ -271,18 +300,23 @@
     )
     arrived(gain_copies)
 
-    arrived(stream_copies)
+    for r in range(1, nd):
+        stream_copies[r - 1].wait_recv()
+        if parts == 2:
+            pair_copies.append(forward(r))
+    arrived(pair_copies)
     squares = jnp.zeros((tokens, 1), jnp.float32)
     for i in range(nd):
-        piece = stream_all[i].astype(jnp.float32)
-        squares = squares + jnp.sum(piece * piece, axis=1, keepdims=True)
+        for c in range(parts):
+            piece = stream_all[c, i].astype(jnp.float32)
+            squares = squares + jnp.sum(piece * piece, axis=1, keepdims=True)
     factor = lax.rsqrt(squares / width + EPSILON)
-    for i in range(nd):
-        start = i * per_dp
+    for i in range(nd * parts):
+        start = i * part
         at = start % per_head
-        gain = gain_all[start // per_head, :, at : at + per_dp]
-        piece = stream_all[i].astype(jnp.float32) * factor * gain
-        normed[:, start : start + per_dp] = piece.astype(jnp.bfloat16)
+        gain = gain_all[start // per_head, :, at : at + part]
+        piece = stream_all[i % parts, i // parts].astype(jnp.float32) * factor * gain
+        normed[:, start : start + part] = piece.astype(jnp.bfloat16)
 
     def hidden_step(n):
         w_in_copy(n).wait()
@@ -315,22 +349,23 @@
         if k < nh - 1:
             slab_copies.append(to_head(2, k + 1, slab_send.at[k], slab_recv.at[k]))
 
-    for j in range(per_head // per_dp):
-        piece = stream_all[h * (per_head // per_dp) + j].astype(jnp.float32)
+    for j in range(per_head // part):
+        source = h * (per_head // per_dp) + j // parts
+        piece = stream_all[j % parts, source].astype(jnp.float32)
         for i in range(nd):
-            own_stream[i, :, j * per_dp : (j + 1) * per_dp] = piece[i * rows : (i + 1) * rows, :]
+            own_stream[i, :, j * part : (j + 1) * part] = piece[i * rows : (i + 1) * rows, :]
 
     arrived(slab_copies)
     summed = total[...]
     for k in range(nh - 1):
         summed = summed + slab_recv[k].astype(jnp.float32)
     for i in range(nd):
-        back_send[i] = summed[i * rows : (i + 1) * rows, :]
+        back_send[i] = summed[i * rows : (i + 1) * rows, :].astype(jnp.bfloat16)
     back_copies = over_dp(4, lambda r: back_send.at[lax.rem(d + r, nd)], back_recv.at[d])
-    result = own_stream[d] + back_send[d]
+    result = own_stream[d] + back_send[d].astype(jnp.float32)
     arrived(back_copies)
     for r in range(1, nd):
-        result = result + back_recv[lax.rem(d + nd - r, nd)]
+        result = result + back_recv[lax.rem(d + nd - r, nd)].astype(jnp.float32)
     out_ref[...] = result.astype(out_ref.dtype)
     for copy in pending:
         copy.wait_send()
@@ -360,6 +395,7 @@
     tokens = nd * rows
     deep, units = w_in.shape[2], w_in.shape[3]
     tile = hidden_tile(units)
+    parts = 2 if nh % 2 == 0 and per_dp % (2 * LANES) == 0 else 1
     f32, bf16 = jnp.float32, jnp.bfloat16
     vmem = pl.BlockSpec(memory_space=pltpu.VMEM)
     smem = pl.BlockSpec(memory_space=pltpu.SMEM)
@@ -373,10 +409,11 @@
         pltpu.VMEM((rows * heads, head_dim), f32),
         pltpu.VMEM((nd, rows, per_head), bf16),
         pltpu.VMEM((nd, rows, LANES), f32),
-        pltpu.VMEM((nd, rows, heads * head_dim), f32),
+        pltpu.VMEM((nd, rows, heads * head_dim), bf16),
         pltpu.VMEM((nh, 1, per_head), f32),
-        pltpu.VMEM((nh, tokens, per_dp), bf16),
-        pltpu.VMEM((nd, tokens, per_dp), bf16),
+        pltpu.VMEM((parts, tokens, per_dp // parts), bf16),
+        pltpu.VMEM((nh, tokens, per_dp // parts), bf16),
+        pltpu.VMEM((parts, nd, tokens, per_dp // parts), bf16),
         pltpu.VMEM((tokens, heads * head_dim), f32),
         pltpu.VMEM((tokens, per_dp), f32),
         pltpu.VMEM((tokens, LANES), f32),
@@ -386,8 +423,8 @@
         pltpu.VMEM((nh - 1, tokens, per_head), bf16),
         pltpu.VMEM((tokens, per_head), f32),
         pltpu.VMEM((nd, rows, per_head), f32),
-        pltpu.VMEM((nd, rows, per_head), f32),
-        pltpu.VMEM((nd, rows, per_head), f32),
+        pltpu.VMEM((nd, rows, per_head), bf16),
+        pltpu.VMEM((nd, rows, per_head), bf16),
         pltpu.SemaphoreType.DMA((2, rows)),
         pltpu.SemaphoreType.DMA,
         pltpu.SemaphoreType.DMA((units // tile,)),
@@ -396,11 +433,13 @@
         pltpu.SemaphoreType.DMA((5, nd)),
         pltpu.SemaphoreType.DMA((3, nh)),
         pltpu.SemaphoreType.DMA((3, nh)),
+        pltpu.SemaphoreType.DMA((nd,)),
+        pltpu.SemaphoreType.DMA((nd,)),
     ]
     return pl.pallas_call(
         functools.partial(layer_kernel, nd, nh),
         out_shape=jax.ShapeDtypeStruct(residual.shape, bf16),
-        in_specs=[vmem] * 4 + [smem] + [vmem] * 4 + [hbm] * 5,
+        in_specs=[vmem] * 4 + [smem] + [vmem] * 2 + [smem] * 2 + [hbm] * 5,
         out_specs=vmem,
         scratch_shapes=scratch,
         compiler_params=pltpu.CompilerParams(
@@ -414,8 +453,8 @@
         lengths,
         pages,
         norm_gain.reshape(1, -1),
-        expert_ids,
-        gate_weights,
+        expert_ids.T,
+        gate_weights.T,
         key_cache,
         value_cache,
         w_out,

time: 56.4 us -> 42.1 us (0.75)
  Pallas kernels: 52.2 us -> 40.5 us
  local copies, waits for them, and re-layouts: 3.98 us -> 1.3 us
    pallas_call x1, Pallas kernels: 52.2 us -> 40.5 us  [shards(): pl.pallas_call(functools.partial(layer_kernel, nd, nh), out_shape=jax.Sha...]
    unnamed x3 -> x1, local copies, waits for them, and re-layouts: 3.98 us -> 1.3 us
where the time goes in v2:
time: 42.1 us; the launch traced here: 41.8 us
  Pallas kernels  40.5 us (96%)
  local copies, waits for them, and re-layouts  1.3 us (3%)
    pallas_call x1, Pallas kernels, shards(): pl.pallas_call(functools.partial(layer_kernel, nd, nh), out_shape=jax.Sha...  40.5 us
    unnamed x1, local copies, waits for them, and re-layouts  1.3 us

profile of v2, /device:TPU:0, one launch (start us, length us, event | category | flops | bytes accessed | tf_op | source)
XLA Modules:
  0.0 41.8 jit_solution(14313725342872474904)
XLA Ops:
  0.0 40.5 %shard_map.136 = bf16[4,1024]{1,0:T(4,128)(2,1)} custom-call(bf16[4,1024]{1,0:T(4,128)(2,1)} %residual_ref.1, bf16[4,8,128]{2,1,0:T(8,128)(2,1)} %query_ref.1, bf16[4,2,128]{2,1,0:T(2,128)(2,1)} %fresh_ref.1, bf16[4,2,128]{2,1,0:T(2,128)(2,1)} %value_new_ref.1, s32[4]{0:T(128)} %lengths_ref.1, s32[4,2,64]{2,1,0:T(2,128)} %pages_ref.1, f32[1,1024]{1,0:T(1,128)} %bitcast.3, ...), custom_call_target="tpu_custom_call" | custom-call | tf_op jit(solution)/shard_map/pallas_call | solution.py:439
  40.5 1.3 %copy.16 = bf16[4,1024]{1,0:T(4,128)(2,1)} copy(bf16[4,1024]{1,0:T(4,128)(2,1)} %shard_map.136) | data formatting | bytes 16384
